TPU v7x, 32 devices: a whole 2x2x4 slice. The times are simulated.
32 devices in a mesh: band: 8 (over z, y), rep: 4 (over x, core).
Axes of the slice: x: 2, y: 2, z: 4, core: 2. Of those that a mesh axis runs over, the one named last changes fastest.
Arguments:
- embeddings: bfloat16 [128, 4096], P('rep', 'band'), may hold values from -6 to 6
- route: int32 [4096, 1], P('band'), may hold values from 0 to 7; in each aligned block of 512 rows (0 to 511, 512 to 1023, ...) at most 160 rows name the same one
- place: bfloat16 [2, 4096], P(None, 'band'), may hold values from 0 to 1
- scales: float32 [4], replicated, may hold values from 0.25 to 1
- first_weight: bfloat16 [512, 512], replicated, may hold values from -0.25 to 0.25
- first_bias: float32 [512], replicated, may hold values from -3 to 3
- second_weight: bfloat16 [512, 512], replicated, may hold values from -0.25 to 0.25
- out_cotangent: bfloat16 [512, 96, 256], P(None, ('band', 'rep')), may hold values from -6 to 6
Outputs:
- embed_gradient: float32 [128, 4096], P('rep', 'band')
- first_weight_gradient: float32 [512, 512], replicated
- first_bias_gradient: float32 [512], replicated
- second_weight_gradient: float32 [512, 512], replicated
Inputs may be any that keep to these rules, and one draw needn't show every extreme that they name: `route`: within the 512 reports of one feed (aligned blocks of rows), at most 160 name the same band, and in some block exactly 160 do.
All inputs are finite; a program needn't handle non-finite values.
Results may differ from a plain program's by a relative error of at most 0.0063.
Values may be sent and summed in bfloat16 or wider, within the bound.
No kernel may reach another device: no remote copies, remote signals or barrier semaphores. Data moves between devices by JAX's collectives and lax.ppermute only.
A program may use at most 128 MiB of HBM per device.

v0:
```python
import jax
import jax.numpy as jnp
from jax import lax
from jax.sharding import PartitionSpec as P

root_two_pi = 0.7978845608028654
cubic = 0.044715


def padded(cells, sides, width):
    for axis, dim in sides:
        count = lax.axis_size(axis)
        ends = count - 1
        head = lax.slice_in_dim(cells, 0, width, axis=dim)
        tail = lax.slice_in_dim(cells, cells.shape[dim] - width, cells.shape[dim], axis=dim)
        cells = jnp.concatenate(
            [
                lax.ppermute(tail, axis, [(i, (i + 1) % count) for i in range(ends)]),
                cells,
                lax.ppermute(head, axis, [((i + 1) % count, i) for i in range(ends)]),
            ],
            axis=dim,
        )
    return cells


def gelu_value(value):
    inner = root_two_pi * (value + cubic * value * value * value)
    return 0.5 * value * (1.0 + jnp.tanh(inner))


def gelu_slope(value):
    tangent = jnp.tanh(root_two_pi * (value + cubic * value * value * value))
    return 0.5 * (1.0 + tangent) + 0.5 * value * (1.0 - tangent * tangent) * root_two_pi * (
        1.0 + 3.0 * cubic * value * value
    )


def kernel_factors(geometry, block, scales, lat_rows, columns):
    north_fraction = geometry[0]
    east_fraction = geometry[1]
    valid = geometry[2]
    centre_rows = jnp.arange(lat_rows, dtype=jnp.float32) + 0.5
    north_gap = (
        ((1 - block).astype(jnp.float32) * lat_rows)[None, :]
        + centre_rows[:, None]
        - (north_fraction * lat_rows)[None, :]
    )
    east_gap = (jnp.arange(columns, dtype=jnp.float32) + 0.5)[:, None] - (east_fraction * columns)[
        None, :
    ]
    reach = scales * lat_rows
    inverse = 0.5 / (reach * reach)
    row_kernel = (
        jnp.exp(-(north_gap * north_gap)[None] * inverse[:, None, None]) * valid[None, None, :]
    ).astype(jnp.bfloat16)
    column_kernel = jnp.exp(-(east_gap * east_gap)[None] * inverse[:, None, None]).astype(
        jnp.bfloat16
    )
    return (row_kernel, column_kernel)


def splat(embedded, row_kernel, column_kernel):
    channels = embedded.shape[0]
    levels, lat_rows, slots = row_kernel.shape
    columns = column_kernel.shape[1]
    sums = []
    weights = []
    for level in range(levels):
        weighted = (embedded[:, None, :] * row_kernel[level][None]).reshape(
            channels * lat_rows, slots
        )
        sums.append(
            lax.dot_general(
                weighted,
                column_kernel[level],
                (((1,), (1,)), ((), ())),
                preferred_element_type=jnp.float32,
            )
        )
        weights.append(
            lax.dot_general(
                row_kernel[level],
                column_kernel[level],
                (((1,), (1,)), ((), ())),
                preferred_element_type=jnp.float32,
            )
        )
    splatted = jnp.stack(sums).reshape(levels, channels, lat_rows * columns)
    density = jnp.stack(weights).reshape(levels, lat_rows * columns)
    features = (
        (splatted / (density[:, None, :] + 1.0))
        .transpose(1, 0, 2)
        .reshape(channels * levels, lat_rows * columns)
        .astype(jnp.bfloat16)
    )
    return (features, density)


def spread_back(gradient, row_kernel, column_kernel):
    levels, lat_rows, slots = row_kernel.shape
    columns = column_kernel.shape[1]
    channels = gradient.shape[0] // levels
    grid = gradient.reshape(channels, levels, lat_rows * columns)
    total = jnp.zeros((channels, slots), jnp.float32)
    for level in range(levels):
        slab = grid[:, level].reshape(channels * lat_rows, columns)
        along = jnp.dot(slab, column_kernel[level], preferred_element_type=jnp.float32).reshape(
            channels, lat_rows, slots
        )
        total = total + jnp.sum(along * row_kernel[level][None].astype(jnp.float32), axis=1)
    return total


def band_ranks(route_rows, bands):
    owner = route_rows[:, 0]
    onehot = (owner[:, None] == jnp.arange(bands, dtype=jnp.int32)[None, :]).astype(jnp.int32)
    running = jnp.cumsum(onehot, axis=0)
    return (owner, jnp.sum((running - 1) * onehot, axis=1))


def on_device(
    embeddings, route, place, scales, first_weight, first_bias, second_weight, out_cotangent
):
    channels, reports = embeddings.shape
    bands = lax.axis_size("band")
    parts = lax.axis_size("rep")
    quarter = lax.axis_index("rep")
    capacity = max(2, 5 * reports // (2 * bands))
    sub_rows = out_cotangent.shape[1]
    lat_rows = sub_rows * parts
    columns = out_cotangent.shape[2]
    levels = scales.shape[0]
    owner, rank = band_ranks(route, bands)
    packed = jnp.concatenate([embeddings, place, jnp.ones((1, reports), jnp.bfloat16)], axis=0)
    rows = channels + 3
    whole = bands * capacity
    outgoing = jnp.zeros((rows, whole), jnp.bfloat16).at[:, owner * capacity + rank].set(packed)
    arrived = lax.all_to_all(outgoing, "band", split_axis=1, concat_axis=1, tiled=True)
    nearby = padded(arrived, (("band", 1),), whole)
    block = jnp.arange(3 * whole, dtype=jnp.int32) // whole
    geometry = nearby[channels:].astype(jnp.float32)
    row_kernel, column_kernel = kernel_factors(geometry, block, scales, lat_rows, columns)
    features, density = splat(nearby[:channels], row_kernel, column_kernel)
    cotangent = out_cotangent.reshape(out_cotangent.shape[0], sub_rows * columns)
    mine = lax.all_to_all(features, "rep", split_axis=1, concat_axis=0, tiled=True)
    local_density = lax.dynamic_slice_in_dim(
        density.reshape(levels, lat_rows, columns), quarter * sub_rows, sub_rows, 1
    ).reshape(levels, sub_rows * columns)
    preact = (
        lax.dot_general(
            first_weight, mine, (((0,), (0,)), ((), ())), preferred_element_type=jnp.float32
        )
        + first_bias[:, None]
    )
    hidden = gelu_value(preact).astype(jnp.bfloat16)
    pre_gradient = (
        jnp.dot(second_weight, cotangent, preferred_element_type=jnp.float32) * gelu_slope(preact)
    ).astype(jnp.bfloat16)
    first_sum = lax.dot_general(
        mine, pre_gradient, (((1,), (1,)), ((), ())), preferred_element_type=jnp.float32
    )
    second_sum = lax.dot_general(
        hidden, cotangent, (((1,), (1,)), ((), ())), preferred_element_type=jnp.float32
    )
    bias_sum = jnp.sum(pre_gradient.astype(jnp.float32), axis=1)
    feature_gradient = jnp.dot(first_weight, pre_gradient, preferred_element_type=jnp.float32)
    count = sub_rows * columns
    cell_part = (
        (feature_gradient.reshape(-1, levels, count) / (local_density[None] + 1.0))
        .reshape(-1, count)
        .astype(jnp.bfloat16)
    )
    splat_gradient = lax.all_to_all(cell_part, "rep", split_axis=0, concat_axis=1, tiled=True)
    totals = lax.psum((first_sum, second_sum, bias_sum), ("band", "rep"))
    slot_gradient = spread_back(splat_gradient, row_kernel, column_kernel)
    outward = jnp.concatenate([slot_gradient[:, :whole], slot_gradient[:, 2 * whole :]], axis=1)
    returned = padded(outward, (("band", 1),), whole)
    own_total = slot_gradient[:, whole : 2 * whole] + returned[:, :whole] + returned[:, 3 * whole :]
    backward = lax.all_to_all(own_total, "band", split_axis=1, concat_axis=1, tiled=True)
    embed_gradient = backward[:, owner * capacity + rank]
    return (embed_gradient, totals[0], totals[2], totals[1])


def solution(mesh):
    return jax.shard_map(
        on_device,
        mesh=mesh,
        in_specs=(
            P("rep", "band"),
            P("band", None),
            P(None, "band"),
            P(),
            P(),
            P(),
            P(),
            P(None, ("band", "rep"), None),
        ),
        out_specs=(P("rep", "band"), P(), P(), P()),
        check_vma=False,
    )
```

profile of v0, /device:TPU:0, one launch (start us, length us, event | category | flops | bytes accessed | tf_op | source)
XLA Modules:
  0.0 270.7 jit_solution(15781892218511032208)
XLA Ops:
  7.9 1.1 reduce-window.6
  11.9 1.9 scatter_custom_fusion
  14.6 7.3 %all-to-all-start = ((bf16[35,8,160]{2,0,1:T(8,128)(2,1)}), bf16[35,8,160]{2,0,1:T(8,128)(2,1)S(1)}, u32[]{:S(2)}, u32[]{:S(2)}) async-start(bf16[35,8,160]{2,0,1:T(8,128)(2,1)} %copy.50), calls=%async_computation | async-start | bytes 327680 | tf_op jit(solution)/shard_map/all_to_all | solution.py:139
  22.6 6.9 %all-to-all-done = bf16[35,8,160]{2,0,1:T(8,128)(2,1)S(1)} async-done(((bf16[35,8,160]{2,0,1:T(8,128)(2,1)}), bf16[35,8,160]{2,0,1:T(8,128)(2,1)S(1)}, u32[]{:S(2)}, u32[]{:S(2)}) %all-to-all-start) | async-done | bytes 89632 | tf_op jit(solution)/shard_map/all_to_all | solution.py:139
  29.7 2.8 %collective-permute-start = (bf16[35,1280]{1,0:T(8,128)(2,1)S(1)}, bf16[35,1280]{1,0:T(8,128)(2,1)S(1)}, u32[]{:S(2)}, u32[]{:S(2)}) collective-permute-start(bf16[35,1280]{1,0:T(8,128)(2,1)S(1)} %all_to_all.42), channel_id=1, source_target_pairs={{0,4},{4,8},{8,12},{12,16},{16,20},{20,24},{24,28},{1,5},{5,9},{9,... | collective-permute-start | bytes 268808 | tf_op jit(solution)/shard_map/ppermute | solution.py:18
  32.6 1.3 collective-permute-start.1
  33.9 2.0 collective-permute-done
  35.8 3.3 %collective-permute-done.1 = bf16[35,1280]{1,0:T(8,128)(2,1)S(1)} collective-permute-done((bf16[35,1280]{1,0:T(8,128)(2,1)S(1)}, bf16[35,1280]{1,0:T(8,128)(2,1)S(1)}, u32[]{:S(2)}, u32[]{:S(2)}) %collective-permute-start.1) | collective-permute-done | bytes 89632 | tf_op jit(solution)/shard_map/ppermute | solution.py:20
  39.6 1.1 fusion.86
  41.2 2.9 %exponential_convert_fusion = bf16[4,256,3840]{2,1,0:T(8,128)(2,1)S(1)} fusion(f32[4]{0:T(128)S(1)} %multiply_divide_fusion, f32[256,3840]{1,0:T(8,128)S(1)} %multiply_negate_fusion), kind=kLoop, calls=%fused_computation.2 | loop fusion | flops 7864320 | bytes 11796496 | tf_op jit(solution)/shard_map/convert_element_type | solution.py:57
  44.7 1.9 fusion.8
  46.6 1.3 fusion.12
  47.9 1.3 fusion.16
  49.2 6.1 %broadcast_multiply_fusion.3 = (bf16[32,12,3840]{2,1,0:T(8,128)(2,1)}, bf16[32,12,3840]{2,1,0:T(8,128)(2,1)}, bf16[32,12,3840]{2,1,0:T(8,128)(2,1)}, bf16[32,12,3840]{2,1,0:T(8,128)(2,1)}) fusion(bf16[12,3840]{1,0:T(8,128)(2,1)S(1)} %copy-done.10, bf16[32,3840]{1,0:T(8,128)(2,1)S(1)} %slice.107, bf16[12,3840]{1,0:T(8,128)(2,1)S(1)} %copy-done.9, ...), kind=kLoop, calls=%fused_computation.33 | loop fusion | flops 5898240 | bytes 12410880 | tf_op jit(solution)/shard_map/mul | solution.py:70
  55.3 3.9 %mul.295 = bf16[384,3840]{1,0:T(8,128)(2,1)S(1)} reshape(bf16[32,12,3840]{2,1,0:T(8,128)(2,1)} %get-tuple-element.39) | data formatting | bytes 5898240 | tf_op jit(solution)/shard_map/mul | solution.py:70
  59.1 3.2 %fusion.18 = f32[384,256]{1,0:T(8,128)} fusion(bf16[384,3840]{1,0:T(8,128)(2,1)S(1)} %mul.295, bf16[4,256,3840]{2,1,0:T(8,128)(2,1)} %copy-done.1), kind=kOutput, calls=%fused_computation.28 | convolution fusion | flops 754974720 | bytes 5308416 | tf_op jit(solution)/shard_map/dot_general | solution.py:74
  62.4 2.1 stack.55
  64.5 3.9 %mul.306 = bf16[384,3840]{1,0:T(8,128)(2,1)S(1)} reshape(bf16[32,12,3840]{2,1,0:T(8,128)(2,1)} %get-tuple-element.40) | data formatting | bytes 5898240 | tf_op jit(solution)/shard_map/mul | solution.py:70
  68.4 3.2 %fusion.14 = f32[384,256]{1,0:T(8,128)} fusion(bf16[384,3840]{1,0:T(8,128)(2,1)S(1)} %mul.306, bf16[4,256,3840]{2,1,0:T(8,128)(2,1)} %copy-done.1), kind=kOutput, calls=%fused_computation.24 | convolution fusion | flops 754974720 | bytes 5308416 | tf_op jit(solution)/shard_map/dot_general | solution.py:74
  71.7 2.2 stack.56
  73.8 3.9 %mul.310 = bf16[384,3840]{1,0:T(8,128)(2,1)S(1)} reshape(bf16[32,12,3840]{2,1,0:T(8,128)(2,1)} %get-tuple-element.41) | data formatting | bytes 5898240 | tf_op jit(solution)/shard_map/mul | solution.py:70
  77.7 3.2 %fusion.10 = f32[384,256]{1,0:T(8,128)} fusion(bf16[384,3840]{1,0:T(8,128)(2,1)S(1)} %mul.310, bf16[4,256,3840]{2,1,0:T(8,128)(2,1)} %copy-done.1), kind=kOutput, calls=%fused_computation.20 | convolution fusion | flops 754974720 | bytes 5308416 | tf_op jit(solution)/shard_map/dot_general | solution.py:74
  81.0 2.1 stack.57
  83.1 3.9 %mul.314 = bf16[384,3840]{1,0:T(8,128)(2,1)S(1)} reshape(bf16[32,12,3840]{2,1,0:T(8,128)(2,1)} %get-tuple-element.42) | data formatting | bytes 5898240 | tf_op jit(solution)/shard_map/mul | solution.py:70
  87.0 3.3 %fusion.6 = f32[384,256]{1,0:T(8,128)} fusion(bf16[384,3840]{1,0:T(8,128)(2,1)S(1)} %mul.314, bf16[4,256,3840]{2,1,0:T(8,128)(2,1)} %copy-done.1), kind=kOutput, calls=%fused_computation.16 | convolution fusion | flops 754974720 | bytes 5308416 | tf_op jit(solution)/shard_map/dot_general | solution.py:74
  90.3 1.4 stack.58
  91.9 2.8 %fusion.54 = bf16[32,4,3072]{2,1,0:T(4,128)(2,1)S(1)} fusion(f32[4,3072]{1,0:T(4,128)S(1)} %maximum_add_fusion, f32[1,32,3072]{2,0,1:T(1,128)S(1)} %stack.58, f32[1,32,3072]{2,0,1:T(1,128)} %stack.57, f32[1,32,3072]{2,0,1:T(1,128)} %stack.56, f32[1,32,3072]{2,0,1:T(1,128)} %stack.55), kind=kLoop, calls=%fused_computation.67 | loop fusion | flops 1966080 | bytes 2408448 | tf_op jit(solution)/shard_map/convert_element_type | solution.py:95
  95.9 3.5 %all-to-all-start.1 = ((bf16[128,4,768]{2,0,1:T(8,128)(2,1)}), bf16[128,4,768]{2,0,1:T(8,128)(2,1)S(1)}, u32[]{:S(2)}, u32[]{:S(2)}) async-start(bf16[128,4,768]{2,0,1:T(8,128)(2,1)} %copy.56), calls=%async_computation.1 | async-start | bytes 1572864 | tf_op jit(solution)/shard_map/all_to_all | solution.py:146
  99.4 1.2 copy.48
  100.9 1.7 div.37
  102.6 8.4 %all-to-all-done.1 = bf16[128,4,768]{2,0,1:T(8,128)(2,1)S(1)} async-done(((bf16[128,4,768]{2,0,1:T(8,128)(2,1)}), bf16[128,4,768]{2,0,1:T(8,128)(2,1)S(1)}, u32[]{:S(2)}, u32[]{:S(2)}) %all-to-all-start.1) | async-done | bytes 786464 | tf_op jit(solution)/shard_map/all_to_all | solution.py:146
  111.7 1.3 convert_reduce_fusion
  113.6 1.5 fusion.39
  115.1 3.5 %all-to-all-start.2 = ((bf16[4,128,768]{2,1,0:T(8,128)(2,1)}), bf16[4,128,768]{2,1,0:T(8,128)(2,1)S(1)}, u32[]{:S(2)}, u32[]{:S(2)}) async-start(bf16[4,128,768]{2,1,0:T(8,128)(2,1)} %bitcast.158), calls=%async_computation.2 | async-start | bytes 1572864 | tf_op jit(solution)/shard_map/all_to_all | solution.py:174
  118.9 2.8 %fusion.90 = f32[512,512]{1,0:T(8,128)} fusion(bf16[512,768]{1,0:T(8,128)(2,1)S(1)} %bitcast.153, bf16[512,768]{1,0:T(8,128)(2,1)} %copy-done.6), kind=kOutput, calls=%fused_computation.140 | convolution fusion | flops 402653184 | bytes 2621440 | tf_op jit(solution)/shard_map/dot_general | solution.py:160
  121.7 1.6 fusion.53
  123.4 6.8 %all-to-all-done.2 = bf16[4,128,768]{2,1,0:T(8,128)(2,1)S(1)} async-done(((bf16[4,128,768]{2,1,0:T(8,128)(2,1)}), bf16[4,128,768]{2,1,0:T(8,128)(2,1)S(1)}, u32[]{:S(2)}, u32[]{:S(2)}) %all-to-all-start.2) | async-done | bytes 786464 | tf_op jit(solution)/shard_map/all_to_all | solution.py:174
  131.2 3.4 %slice_reduce_fusion.2 = (bf16[32,3072]{1,0:T(8,128)(2,1)S(1)}, bf16[32,3072]{1,0:T(8,128)(2,1)S(1)}, bf16[32,3072]{1,0:T(8,128)(2,1)S(1)}, bf16[32,3072]{1,0:T(8,128)(2,1)S(1)}) fusion(bf16[32,4,3072]{2,1,0:T(4,128)(2,1)S(1)} %reshape.284), kind=kLoop, calls=%fused_computation.71 | loop fusion | bytes 1572864 | tf_op jit(solution)/shard_map/slice | solution.py:107
  134.6 2.7 %fusion.23 = f32[32,3840]{1,0:T(8,128)S(1)} fusion(f32[12,3840]{1,0:T(8,128)S(1)} %copy-done.14, bf16[4,256,3840]{2,1,0:T(8,128)(2,1)} %copy-done.1, bf16[4,12,8,256]{3,2,1,0:T(8,128)(2,1)S(1)} %bitcast.163), kind=kOutput, calls=%fused_computation.35 | convolution fusion | flops 757800960 | bytes 2838528 | tf_op jit(solution)/shard_map/dot_general | solution.py:108
  137.3 2.6 fusion.20
  142.1 3.6 %collective-permute-start.2 = (f32[32,1280]{1,0:T(8,128)S(1)}, f32[32,1280]{1,0:T(8,128)S(1)}, u32[]{:S(2)}, u32[]{:S(2)}) collective-permute-start(f32[32,1280]{1,0:T(8,128)S(1)} %get-tuple-element.29), channel_id=1, source_target_pairs={{0,4},{4,8},{8,12},{12,16},{16,20},{20,24},{24,28},{1,5},{5,9},{9,... | collective-permute-start | bytes 491528 | tf_op jit(solution)/shard_map/ppermute | solution.py:18
  145.7 1.3 collective-permute-start.3
  147.0 3.3 %collective-permute-done.2 = f32[32,1280]{1,0:T(8,128)S(1)} collective-permute-done((f32[32,1280]{1,0:T(8,128)S(1)}, f32[32,1280]{1,0:T(8,128)S(1)}, u32[]{:S(2)}, u32[]{:S(2)}) %collective-permute-start.2) | collective-permute-done | bytes 163872 | tf_op jit(solution)/shard_map/ppermute | solution.py:18
  150.3 2.6 collective-permute-done.3
  153.9 5.2 %all-to-all-start.3 = ((f32[32,8,160]{2,0,1:T(8,128)}), f32[32,8,160]{2,0,1:T(8,128)S(1)}, u32[]{:S(2)}, u32[]{:S(2)}) async-start(f32[32,8,160]{2,0,1:T(8,128)} %copy.63), calls=%async_computation.3 | async-start | bytes 524288 | tf_op jit(solution)/shard_map/all_to_all | solution.py:180
  159.2 40.6 %psum.22 = f32[512]{0:T(512)} all-reduce(f32[512]{0:T(512)S(1)} %get-tuple-element.43), channel_id=1, replica_groups=mesh['band'=8,'rep'=4] {'band','rep'}, use_global_device_ids=true, to_apply=%region_10.11 | all-reduce | flops 512 | bytes 4096 | tf_op jit(solution)/shard_map/psum | solution.py:175
  201.9 58.7 %all-reduce.3.cloned.1.call-done = (f32[512,512]{1,0:T(8,128)}, f32[512,512]{1,0:T(8,128)}) async-done(((f32[512,512]{1,0:T(8,128)}, f32[512,512]{1,0:T(8,128)}), (f32[512,512]{1,0:T(8,128)}, f32[512,512]{1,0:T(8,128)})) %all-reduce.3.cloned.1.call-update) | async-done | bytes 2097168 | tf_op jit(solution)/shard_map/psum | solution.py:175
  260.6 2.4 copy.96
  (107 shorter events, 17.0 us)
Async XLA Ops:
  7.2 103.8 %copy-start = (bf16[512,512]{1,0:T(8,128)(2,1)S(1)}, bf16[512,512]{1,0:T(8,128)(2,1)}, u32[]{:S(2)}) copy-start(bf16[512,512]{1,0:T(8,128)(2,1)} %param.12) | copy-start | bytes 1572868
  10.8 28.9 %copy-start.18 = (s32[512,1]{0,1:T(1,128)}, s32[512,1]{0,1:T(1,128)S(1)}, u32[]{:S(2)}) copy-start(s32[512,1]{0,1:T(1,128)S(1)} %compare_select_fusion) | copy-start | bytes 6148
  14.6 14.9 %all-to-all-start = ((bf16[35,8,160]{2,0,1:T(8,128)(2,1)}), bf16[35,8,160]{2,0,1:T(8,128)(2,1)S(1)}, u32[]{:S(2)}, u32[]{:S(2)}) async-start(bf16[35,8,160]{2,0,1:T(8,128)(2,1)} %copy.50), calls=%async_computation | async-start | bytes 327680 | tf_op jit(solution)/shard_map/all_to_all | solution.py:139
  29.7 6.1 %collective-permute-start = (bf16[35,1280]{1,0:T(8,128)(2,1)S(1)}, bf16[35,1280]{1,0:T(8,128)(2,1)S(1)}, u32[]{:S(2)}, u32[]{:S(2)}) collective-permute-start(bf16[35,1280]{1,0:T(8,128)(2,1)S(1)} %all_to_all.42), channel_id=1, source_target_pairs={{0,4},{4,8},{8,12},{12,16},{16,20},{20,24},{24,28},{1,5},{5,9},{9,... | collective-permute-start | bytes 268808 | tf_op jit(solution)/shard_map/ppermute | solution.py:18
  32.6 6.6 %collective-permute-start.1 = (bf16[35,1280]{1,0:T(8,128)(2,1)S(1)}, bf16[35,1280]{1,0:T(8,128)(2,1)S(1)}, u32[]{:S(2)}, u32[]{:S(2)}) collective-permute-start(bf16[35,1280]{1,0:T(8,128)(2,1)S(1)} %all_to_all.42), channel_id=1, source_target_pairs={{4,0},{8,4},{12,8},{16,12},{20,16},{24,20},{28,24},{5,1},{9,5},{13... | collective-permute-start | bytes 268808 | tf_op jit(solution)/shard_map/ppermute | solution.py:20
  44.2 11.1 %copy-start.1 = (bf16[4,256,3840]{2,1,0:T(8,128)(2,1)}, bf16[4,256,3840]{2,1,0:T(8,128)(2,1)S(1)}, u32[]{:S(2)}) copy-start(bf16[4,256,3840]{2,1,0:T(8,128)(2,1)S(1)} %exponential_convert_fusion) | copy-start | bytes 23592964
  46.6 2.5 copy-start.7
  46.6 2.5 copy-start.8
  46.6 2.5 copy-start.9
  46.6 2.5 copy-start.10
  87.0 4.7 %copy-start.15 = (f32[12,256]{1,0:T(8,128)S(1)}, f32[12,256]{1,0:T(8,128)}, u32[]{:S(2)}) copy-start(f32[12,256]{1,0:T(8,128)} %fusion.8) | copy-start | bytes 36868
  87.0 4.7 %copy-start.16 = (f32[12,256]{1,0:T(8,128)S(1)}, f32[12,256]{1,0:T(8,128)}, u32[]{:S(2)}) copy-start(f32[12,256]{1,0:T(8,128)} %fusion.12) | copy-start | bytes 36868
  87.0 4.8 %copy-start.17 = (f32[12,256]{1,0:T(8,128)S(1)}, f32[12,256]{1,0:T(8,128)}, u32[]{:S(2)}) copy-start(f32[12,256]{1,0:T(8,128)} %fusion.16) | copy-start | bytes 36868
  94.9 4.5 %copy-start.4 = (bf16[512,3,256]{2,0,1:T(8,128)(2,1)S(1)}, bf16[512,3,256]{2,0,1:T(8,128)(2,1)}, u32[]{:S(2)}) copy-start(bf16[512,3,256]{2,0,1:T(8,128)(2,1)} %param.15) | copy-start | bytes 2359300
  95.9 15.1 %all-to-all-start.1 = ((bf16[128,4,768]{2,0,1:T(8,128)(2,1)}), bf16[128,4,768]{2,0,1:T(8,128)(2,1)S(1)}, u32[]{:S(2)}, u32[]{:S(2)}) async-start(bf16[128,4,768]{2,0,1:T(8,128)(2,1)} %copy.56), calls=%async_computation.1 | async-start | bytes 1572864 | tf_op jit(solution)/shard_map/all_to_all | solution.py:146
  100.8 10.2 %copy-start.21 = (f32[512]{0:T(512)S(1)}, f32[512]{0:T(512)}, u32[]{:S(2)}) copy-start(f32[512]{0:T(512)} %param.13) | copy-start | bytes 6148
  102.6 9.1 %copy-start.5 = (bf16[512,3,256]{0,2,1:T(8,128)(2,1)S(1)}, bf16[512,3,256]{0,2,1:T(8,128)(2,1)}, u32[]{:S(2)}) copy-start(bf16[512,3,256]{0,2,1:T(8,128)(2,1)} %copy.48) | copy-start | bytes 2359300
  102.6 9.1 %copy-start.20 = (bf16[512,512]{1,0:T(8,128)(2,1)S(1)}, bf16[512,512]{1,0:T(8,128)(2,1)}, u32[]{:S(2)}) copy-start(bf16[512,512]{1,0:T(8,128)(2,1)} %param.14) | copy-start | bytes 1572868
  111.6 1.4 copy-start.22
  111.7 2.0 copy-start.2
  113.0 2.1 copy-start.6
  115.1 15.1 %all-to-all-start.2 = ((bf16[4,128,768]{2,1,0:T(8,128)(2,1)}), bf16[4,128,768]{2,1,0:T(8,128)(2,1)S(1)}, u32[]{:S(2)}, u32[]{:S(2)}) async-start(bf16[4,128,768]{2,1,0:T(8,128)(2,1)} %bitcast.158), calls=%async_computation.2 | async-start | bytes 1572864 | tf_op jit(solution)/shard_map/all_to_all | solution.py:174
  118.6 141.9 %all-reduce.3.cloned.1.call-start = ((), (), s32[]{:S(2)}) async-start(), calls=%async_computation.4 | async-start | bytes 4194304 | tf_op jit(solution)/shard_map/psum | solution.py:175
  118.9 2.8 %copy-start.23 = (f32[768,512]{0,1:T(8,128)S(1)}, f32[768,512]{0,1:T(8,128)}, u32[]{:S(2)}) copy-start(f32[768,512]{0,1:T(8,128)} %copy-done.22) | copy-start | bytes 4718596
  130.8 3.7 %copy-start.14 = (f32[12,3840]{1,0:T(8,128)S(1)}, f32[12,3840]{1,0:T(8,128)}, u32[]{:S(2)}) copy-start(f32[12,3840]{1,0:T(8,128)} %get-tuple-element.31) | copy-start | bytes 552964
  131.1 8.8 %slice-start = ((s8[7864320]{0:T(1024)(128)(4,1)}), s8[3670016]{0:T(1024)(128)(4,1)S(1)}, s32[]{:S(2)}) async-start(s8[7864320]{0:T(1024)(128)(4,1)} %bitcast.149), calls=%async_computation.5 | async-start | bytes 7340032
  134.6 2.7 %copy-start.13 = (f32[12,3840]{1,0:T(8,128)S(1)}, f32[12,3840]{1,0:T(8,128)}, u32[]{:S(2)}) copy-start(f32[12,3840]{1,0:T(8,128)} %get-tuple-element.34) | copy-start | bytes 552964
  134.6 5.4 %slice-start.1 = ((s8[7864320]{0:T(1024)(128)(4,1)}), s8[4194304]{0:T(1024)(128)(4,1)S(1)}, s32[]{:S(2)}) async-start(s8[7864320]{0:T(1024)(128)(4,1)} %bitcast.149), calls=%async_computation.6 | async-start | bytes 8388608
  137.3 2.6 copy-start.12
  140.0 1.0 copy-start.11
  142.0 17.1 %copy-start.19 = (s32[512,1]{0,1:T(1,128)S(1)}, s32[512,1]{0,1:T(1,128)}, u32[]{:S(2)}) copy-start(s32[512,1]{0,1:T(1,128)} %copy-done.18) | copy-start | bytes 6148
  142.1 8.3 %collective-permute-start.2 = (f32[32,1280]{1,0:T(8,128)S(1)}, f32[32,1280]{1,0:T(8,128)S(1)}, u32[]{:S(2)}, u32[]{:S(2)}) collective-permute-start(f32[32,1280]{1,0:T(8,128)S(1)} %get-tuple-element.29), channel_id=1, source_target_pairs={{0,4},{4,8},{8,12},{12,16},{16,20},{20,24},{24,28},{1,5},{5,9},{9,... | collective-permute-start | bytes 491528 | tf_op jit(solution)/shard_map/ppermute | solution.py:18
  145.7 7.3 %collective-permute-start.3 = (f32[32,1280]{1,0:T(8,128)S(1)}, f32[32,1280]{1,0:T(8,128)S(1)}, u32[]{:S(2)}, u32[]{:S(2)}) collective-permute-start(f32[32,1280]{1,0:T(8,128)S(1)} %get-tuple-element.30), channel_id=1, source_target_pairs={{4,0},{8,4},{12,8},{16,12},{20,16},{24,20},{28,24},{5,1},{9,5},{13... | collective-permute-start | bytes 491528 | tf_op jit(solution)/shard_map/ppermute | solution.py:20
  153.9 45.9 %all-to-all-start.3 = ((f32[32,8,160]{2,0,1:T(8,128)}), f32[32,8,160]{2,0,1:T(8,128)S(1)}, u32[]{:S(2)}, u32[]{:S(2)}) async-start(f32[32,8,160]{2,0,1:T(8,128)} %copy.63), calls=%async_computation.3 | async-start | bytes 524288 | tf_op jit(solution)/shard_map/all_to_all | solution.py:180
  260.6 2.4 copy-start.3
Sparse Core Ops, SparseCore 0:
  125.5 134.9 all-reduce.2
where the time goes:
time: 272 us; the launch traced here: 271 us
  waiting for transfers between devices  92.1 us (34%)
  local copies, waits for them, and re-layouts  42.5 us (16%)
  blocking collectives  40.6 us (15%)
  matrix products  33.1 us (12%)
  starting transfers between devices  28.8 us (11%)
  other arithmetic  18.9 us (7%)
  between operations  14.7 us (5%)
    psum x1, waiting for transfers between devices, on_device(): totals = lax.psum((first_sum, second_sum, bias_sum), ('band', 'rep'))  58.7 us
    psum x1, blocking collectives, on_device(): totals = lax.psum((first_sum, second_sum, bias_sum), ('band', 'rep'))  40.6 us
    mul x4, local copies, waits for them, and re-layouts, splat(): embedded[:, None, :] * row_kernel[level][None]  15.5 us
    dot_general x4, matrix products, splat(): lax.dot_general(weighted, column_kernel[level], (((1,), (1,)), ((), ())),...  13 us
    all_to_all x1, waiting for transfers between devices, on_device(): lax.all_to_all(features, 'rep', split_axis=1, concat_axis=0, tiled=True)  8.44 us
    another operation x4, local copies, waits for them, and re-layouts, splat(): splatted = jnp.stack(sums).reshape(levels, channels, lat_rows * columns)  7.83 us
    all_to_all x1, starting transfers between devices, on_device(): lax.all_to_all(outgoing, 'band', split_axis=1, concat_axis=1, tiled=True)  7.31 us
    dot_general x4, matrix products, spread_back(): jnp.dot(slab, column_kernel[level], preferred_element_type=jnp.float32)  7.24 us
  transfers between devices with their start and end apart: 9, of which 8 were waited for; matrix products, arithmetic and copies ran while one was open for 8% of the time, Pallas kernels for 0%

commit v1 on v0

--- a/solution.py
+++ b/solution.py
@@ -172,7 +172,7 @@
         .astype(jnp.bfloat16)
     )
     splat_gradient = lax.all_to_all(cell_part, "rep", split_axis=0, concat_axis=1, tiled=True)
-    totals = lax.psum((first_sum, second_sum, bias_sum), ("band", "rep"))
+    totals = lax.psum(lax.psum((first_sum, second_sum, bias_sum), "rep"), "band")
     slot_gradient = spread_back(splat_gradient, row_kernel, column_kernel)
     outward = jnp.concatenate([slot_gradient[:, :whole], slot_gradient[:, 2 * whole :]], axis=1)
     returned = padded(outward, (("band", 1),), whole)

time: 272 us -> 297 us (1.092)
  waiting for transfers between devices: 92.1 us -> 127 us
  blocking collectives: 40.6 us -> 29 us
    psum x1 -> x2, waiting for transfers between devices: 58.7 us -> 93.2 us  [the longest x1 61.7 us: on_device(): lax.psum(lax.psum((first_sum, second_sum, bias_sum), 'rep'), 'band')]
    psum x1 -> x2, blocking collectives: 40.6 us -> 29 us  [the longest x1 22.9 us: on_device(): lax.psum(lax.psum((first_sum, second_sum, bias_sum), 'rep'), 'band')]
  transfers between devices with their start and end apart: 9 -> 10, of which waited for: 8 -> 9; matrix products, arithmetic and copies ran while one was open for 8% -> 8% of each run, Pallas kernels for 0% -> 0%
where the time goes in v1:
time: 297 us; the launch traced here: 296 us
  waiting for transfers between devices  127 us (43%)
  local copies, waits for them, and re-layouts  42.5 us (14%)
  matrix products  33.1 us (11%)
  starting transfers between devices  30.6 us (10%)
  blocking collectives  29 us (10%)
  other arithmetic  18.9 us (6%)
  between operations  14.7 us (5%)
    psum x1, waiting for transfers between devices, on_device(): lax.psum(lax.psum((first_sum, second_sum, bias_sum), 'rep'), 'band')  61.7 us
    psum x1, waiting for transfers between devices, on_device(): lax.psum((first_sum, second_sum, bias_sum), 'rep')  31.6 us
    psum x1, blocking collectives, on_device(): lax.psum(lax.psum((first_sum, second_sum, bias_sum), 'rep'), 'band')  22.9 us
    mul x4, local copies, waits for them, and re-layouts, splat(): embedded[:, None, :] * row_kernel[level][None]  15.5 us
    dot_general x4, matrix products, splat(): lax.dot_general(weighted, column_kernel[level], (((1,), (1,)), ((), ())),...  13 us
    all_to_all x1, waiting for transfers between devices, on_device(): lax.all_to_all(features, 'rep', split_axis=1, concat_axis=0, tiled=True)  8.44 us
    another operation x4, local copies, waits for them, and re-layouts, splat(): splatted = jnp.stack(sums).reshape(levels, channels, lat_rows * columns)  7.83 us
    ppermute x2, waiting for transfers between devices, padded(): lax.ppermute(head, axis, [((i + 1) % count, i) for i in range(ends)])  7.38 us
  transfers between devices with their start and end apart: 10, of which 9 were waited for; matrix products, arithmetic and copies ran while one was open for 8% of the time, Pallas kernels for 0%

profile of v1, /device:TPU:0, one launch (start us, length us, event | category | flops | bytes accessed | tf_op | source)
XLA Modules:
  0.0 295.9 jit_solution(13367626096090955548)
XLA Ops:
  11.9 1.9 scatter_custom_fusion
  14.6 7.3 %all-to-all-start = ((bf16[35,8,160]{2,0,1:T(8,128)(2,1)}), bf16[35,8,160]{2,0,1:T(8,128)(2,1)S(1)}, u32[]{:S(2)}, u32[]{:S(2)}) async-start(bf16[35,8,160]{2,0,1:T(8,128)(2,1)} %copy.50), calls=%async_computation | async-start | bytes 327680 | tf_op jit(solution)/shard_map/all_to_all | solution.py:139
  22.6 6.9 %all-to-all-done = bf16[35,8,160]{2,0,1:T(8,128)(2,1)S(1)} async-done(((bf16[35,8,160]{2,0,1:T(8,128)(2,1)}), bf16[35,8,160]{2,0,1:T(8,128)(2,1)S(1)}, u32[]{:S(2)}, u32[]{:S(2)}) %all-to-all-start) | async-done | bytes 89632 | tf_op jit(solution)/shard_map/all_to_all | solution.py:139
  29.7 2.8 collective-permute-start
  32.6 1.3 collective-permute-start.1
  33.9 2.0 collective-permute-done
  35.8 3.3 %collective-permute-done.1 = bf16[35,1280]{1,0:T(8,128)(2,1)S(1)} collective-permute-done((bf16[35,1280]{1,0:T(8,128)(2,1)S(1)}, bf16[35,1280]{1,0:T(8,128)(2,1)S(1)}, u32[]{:S(2)}, u32[]{:S(2)}) %collective-permute-start.1) | collective-permute-done | bytes 89632 | tf_op jit(solution)/shard_map/ppermute | solution.py:20
  41.2 2.9 exponential_convert_fusion
  44.7 1.9 fusion.8
  46.6 1.3 fusion.12
  47.9 1.3 fusion.16
  49.2 6.1 %broadcast_multiply_fusion.3 = (bf16[32,12,3840]{2,1,0:T(8,128)(2,1)}, bf16[32,12,3840]{2,1,0:T(8,128)(2,1)}, bf16[32,12,3840]{2,1,0:T(8,128)(2,1)}, bf16[32,12,3840]{2,1,0:T(8,128)(2,1)}) fusion(bf16[12,3840]{1,0:T(8,128)(2,1)S(1)} %copy-done.10, bf16[32,3840]{1,0:T(8,128)(2,1)S(1)} %slice.107, bf16[12,3840]{1,0:T(8,128)(2,1)S(1)} %copy-done.9, ...), kind=kLoop, calls=%fused_computation.33 | loop fusion | flops 5898240 | bytes 12410880 | tf_op jit(solution)/shard_map/mul | solution.py:70
  55.3 3.9 %mul.295 = bf16[384,3840]{1,0:T(8,128)(2,1)S(1)} reshape(bf16[32,12,3840]{2,1,0:T(8,128)(2,1)} %get-tuple-element.41) | data formatting | bytes 5898240 | tf_op jit(solution)/shard_map/mul | solution.py:70
  59.1 3.2 %fusion.18 = f32[384,256]{1,0:T(8,128)} fusion(bf16[384,3840]{1,0:T(8,128)(2,1)S(1)} %mul.295, bf16[4,256,3840]{2,1,0:T(8,128)(2,1)} %copy-done.1), kind=kOutput, calls=%fused_computation.28 | convolution fusion | flops 754974720 | bytes 5308416 | tf_op jit(solution)/shard_map/dot_general | solution.py:74
  62.4 2.1 stack.55
  64.5 3.9 %mul.306 = bf16[384,3840]{1,0:T(8,128)(2,1)S(1)} reshape(bf16[32,12,3840]{2,1,0:T(8,128)(2,1)} %get-tuple-element.42) | data formatting | bytes 5898240 | tf_op jit(solution)/shard_map/mul | solution.py:70
  68.4 3.2 %fusion.14 = f32[384,256]{1,0:T(8,128)} fusion(bf16[384,3840]{1,0:T(8,128)(2,1)S(1)} %mul.306, bf16[4,256,3840]{2,1,0:T(8,128)(2,1)} %copy-done.1), kind=kOutput, calls=%fused_computation.24 | convolution fusion | flops 754974720 | bytes 5308416 | tf_op jit(solution)/shard_map/dot_general | solution.py:74
  71.7 2.2 stack.56
  73.8 3.9 %mul.310 = bf16[384,3840]{1,0:T(8,128)(2,1)S(1)} reshape(bf16[32,12,3840]{2,1,0:T(8,128)(2,1)} %get-tuple-element.43) | data formatting | bytes 5898240 | tf_op jit(solution)/shard_map/mul | solution.py:70
  77.7 3.2 %fusion.10 = f32[384,256]{1,0:T(8,128)} fusion(bf16[384,3840]{1,0:T(8,128)(2,1)S(1)} %mul.310, bf16[4,256,3840]{2,1,0:T(8,128)(2,1)} %copy-done.1), kind=kOutput, calls=%fused_computation.20 | convolution fusion | flops 754974720 | bytes 5308416 | tf_op jit(solution)/shard_map/dot_general | solution.py:74
  81.0 2.1 stack.57
  83.1 3.9 %mul.314 = bf16[384,3840]{1,0:T(8,128)(2,1)S(1)} reshape(bf16[32,12,3840]{2,1,0:T(8,128)(2,1)} %get-tuple-element.44) | data formatting | bytes 5898240 | tf_op jit(solution)/shard_map/mul | solution.py:70
  87.0 3.3 %fusion.6 = f32[384,256]{1,0:T(8,128)} fusion(bf16[384,3840]{1,0:T(8,128)(2,1)S(1)} %mul.314, bf16[4,256,3840]{2,1,0:T(8,128)(2,1)} %copy-done.1), kind=kOutput, calls=%fused_computation.16 | convolution fusion | flops 754974720 | bytes 5308416 | tf_op jit(solution)/shard_map/dot_general | solution.py:74
  90.3 1.4 stack.58
  91.9 2.8 fusion.54
  95.9 3.5 %all-to-all-start.1 = ((bf16[128,4,768]{2,0,1:T(8,128)(2,1)}), bf16[128,4,768]{2,0,1:T(8,128)(2,1)S(1)}, u32[]{:S(2)}, u32[]{:S(2)}) async-start(bf16[128,4,768]{2,0,1:T(8,128)(2,1)} %copy.56), calls=%async_computation.1 | async-start | bytes 1572864 | tf_op jit(solution)/shard_map/all_to_all | solution.py:146
  99.4 1.2 copy.48
  100.9 1.7 div.37
  102.6 8.4 %all-to-all-done.1 = bf16[128,4,768]{2,0,1:T(8,128)(2,1)S(1)} async-done(((bf16[128,4,768]{2,0,1:T(8,128)(2,1)}), bf16[128,4,768]{2,0,1:T(8,128)(2,1)S(1)}, u32[]{:S(2)}, u32[]{:S(2)}) %all-to-all-start.1) | async-done | bytes 786464 | tf_op jit(solution)/shard_map/all_to_all | solution.py:146
  111.7 1.3 convert_reduce_fusion
  113.6 1.5 fusion.39
  115.1 3.5 %all-to-all-start.2 = ((bf16[4,128,768]{2,1,0:T(8,128)(2,1)}), bf16[4,128,768]{2,1,0:T(8,128)(2,1)S(1)}, u32[]{:S(2)}, u32[]{:S(2)}) async-start(bf16[4,128,768]{2,1,0:T(8,128)(2,1)} %bitcast.158), calls=%async_computation.2 | async-start | bytes 1572864 | tf_op jit(solution)/shard_map/all_to_all | solution.py:174
  118.9 2.8 fusion.90
  121.7 1.6 fusion.53
  123.4 7.3 %all-to-all-done.2 = bf16[4,128,768]{2,1,0:T(8,128)(2,1)S(1)} async-done(((bf16[4,128,768]{2,1,0:T(8,128)(2,1)}), bf16[4,128,768]{2,1,0:T(8,128)(2,1)S(1)}, u32[]{:S(2)}, u32[]{:S(2)}) %all-to-all-start.2) | async-done | bytes 786464 | tf_op jit(solution)/shard_map/all_to_all | solution.py:174
  131.6 3.4 %slice_reduce_fusion.2 = (bf16[32,3072]{1,0:T(8,128)(2,1)S(1)}, bf16[32,3072]{1,0:T(8,128)(2,1)S(1)}, bf16[32,3072]{1,0:T(8,128)(2,1)S(1)}, bf16[32,3072]{1,0:T(8,128)(2,1)S(1)}) fusion(bf16[32,4,3072]{2,1,0:T(4,128)(2,1)S(1)} %reshape.284), kind=kLoop, calls=%fused_computation.71 | loop fusion | bytes 1572864 | tf_op jit(solution)/shard_map/slice | solution.py:107
  135.1 2.7 fusion.23
  137.8 2.6 fusion.20
  142.4 31.6 %all-reduce.7.cloned.1.call-done = (f32[512,512]{1,0:T(8,128)}, f32[512,512]{1,0:T(8,128)}) async-done(((f32[512,512]{1,0:T(8,128)}, f32[512,512]{1,0:T(8,128)}), (f32[512,512]{1,0:T(8,128)}, f32[512,512]{1,0:T(8,128)})) %all-reduce.7.cloned.1.call-update) | async-done | bytes 2097168 | tf_op jit(solution)/shard_map/psum | solution.py:175
  174.1 3.4 %collective-permute-start.2 = (f32[32,1280]{1,0:T(8,128)S(1)}, f32[32,1280]{1,0:T(8,128)S(1)}, u32[]{:S(2)}, u32[]{:S(2)}) collective-permute-start(f32[32,1280]{1,0:T(8,128)S(1)} %get-tuple-element.31), channel_id=1, source_target_pairs={{0,4},{4,8},{8,12},{12,16},{16,20},{20,24},{24,28},{1,5},{5,9},{9,... | collective-permute-start | bytes 491528 | tf_op jit(solution)/shard_map/ppermute | solution.py:18
  177.5 1.3 collective-permute-start.3
  178.8 1.9 collective-permute-done.2
  180.7 4.1 %collective-permute-done.3 = f32[32,1280]{1,0:T(8,128)S(1)} collective-permute-done((f32[32,1280]{1,0:T(8,128)S(1)}, f32[32,1280]{1,0:T(8,128)S(1)}, u32[]{:S(2)}, u32[]{:S(2)}) %collective-permute-start.3) | collective-permute-done | bytes 163872 | tf_op jit(solution)/shard_map/ppermute | solution.py:20
  185.8 7.2 %all-to-all-start.3 = ((f32[32,8,160]{2,0,1:T(8,128)}), f32[32,8,160]{2,0,1:T(8,128)S(1)}, u32[]{:S(2)}, u32[]{:S(2)}) async-start(f32[32,8,160]{2,0,1:T(8,128)} %copy.63), calls=%async_computation.3 | async-start | bytes 524288 | tf_op jit(solution)/shard_map/all_to_all | solution.py:180
  193.0 6.1 %psum.44 = f32[512]{0:T(512)S(1)} all-reduce(f32[512]{0:T(512)S(1)} %get-tuple-element.45), channel_id=1, replica_groups=mesh['band'=8,'rep'=4] {'rep'}, use_global_device_ids=true, to_apply=%region_11.12 | all-reduce | flops 512 | bytes 4096 | tf_op jit(solution)/shard_map/psum | solution.py:175
  199.1 22.9 %psum.45 = f32[512]{0:T(512)} all-reduce(f32[512]{0:T(512)S(1)} %psum.44), channel_id=1, replica_groups=mesh['band'=8,'rep'=4] {'band'}, use_global_device_ids=true, to_apply=%region_12.13 | all-reduce | flops 512 | bytes 4096 | tf_op jit(solution)/shard_map/psum | solution.py:175
  224.1 61.7 %all-reduce.5.cloned.1.call-done = (f32[512,512]{1,0:T(8,128)}, f32[512,512]{1,0:T(8,128)}) async-done(((f32[512,512]{1,0:T(8,128)}, f32[512,512]{1,0:T(8,128)}), (f32[512,512]{1,0:T(8,128)}, f32[512,512]{1,0:T(8,128)})) %all-reduce.5.cloned.1.call-update) | async-done | bytes 2097168 | tf_op jit(solution)/shard_map/psum | solution.py:175
  285.8 2.4 copy.98
  (111 shorter events, 19.3 us)
Async XLA Ops:
  7.2 103.8 %copy-start = (bf16[512,512]{1,0:T(8,128)(2,1)S(1)}, bf16[512,512]{1,0:T(8,128)(2,1)}, u32[]{:S(2)}) copy-start(bf16[512,512]{1,0:T(8,128)(2,1)} %param.12) | copy-start | bytes 1572868
  10.8 28.9 %copy-start.18 = (s32[512,1]{0,1:T(1,128)}, s32[512,1]{0,1:T(1,128)S(1)}, u32[]{:S(2)}) copy-start(s32[512,1]{0,1:T(1,128)S(1)} %compare_select_fusion) | copy-start | bytes 6148
  14.6 14.9 %all-to-all-start = ((bf16[35,8,160]{2,0,1:T(8,128)(2,1)}), bf16[35,8,160]{2,0,1:T(8,128)(2,1)S(1)}, u32[]{:S(2)}, u32[]{:S(2)}) async-start(bf16[35,8,160]{2,0,1:T(8,128)(2,1)} %copy.50), calls=%async_computation | async-start | bytes 327680 | tf_op jit(solution)/shard_map/all_to_all | solution.py:139
  29.7 6.1 %collective-permute-start = (bf16[35,1280]{1,0:T(8,128)(2,1)S(1)}, bf16[35,1280]{1,0:T(8,128)(2,1)S(1)}, u32[]{:S(2)}, u32[]{:S(2)}) collective-permute-start(bf16[35,1280]{1,0:T(8,128)(2,1)S(1)} %all_to_all.42), channel_id=1, source_target_pairs={{0,4},{4,8},{8,12},{12,16},{16,20},{20,24},{24,28},{1,5},{5,9},{9,... | collective-permute-start | bytes 268808 | tf_op jit(solution)/shard_map/ppermute | solution.py:18
  32.6 6.6 %collective-permute-start.1 = (bf16[35,1280]{1,0:T(8,128)(2,1)S(1)}, bf16[35,1280]{1,0:T(8,128)(2,1)S(1)}, u32[]{:S(2)}, u32[]{:S(2)}) collective-permute-start(bf16[35,1280]{1,0:T(8,128)(2,1)S(1)} %all_to_all.42), channel_id=1, source_target_pairs={{4,0},{8,4},{12,8},{16,12},{20,16},{24,20},{28,24},{5,1},{9,5},{13... | collective-permute-start | bytes 268808 | tf_op jit(solution)/shard_map/ppermute | solution.py:20
  44.2 11.1 %copy-start.1 = (bf16[4,256,3840]{2,1,0:T(8,128)(2,1)}, bf16[4,256,3840]{2,1,0:T(8,128)(2,1)S(1)}, u32[]{:S(2)}) copy-start(bf16[4,256,3840]{2,1,0:T(8,128)(2,1)S(1)} %exponential_convert_fusion) | copy-start | bytes 23592964
  46.6 2.5 copy-start.7
  46.6 2.5 copy-start.8
  46.6 2.5 copy-start.9
  46.6 2.5 copy-start.10
  87.0 4.7 %copy-start.15 = (f32[12,256]{1,0:T(8,128)S(1)}, f32[12,256]{1,0:T(8,128)}, u32[]{:S(2)}) copy-start(f32[12,256]{1,0:T(8,128)} %fusion.8) | copy-start | bytes 36868
  87.0 4.7 %copy-start.16 = (f32[12,256]{1,0:T(8,128)S(1)}, f32[12,256]{1,0:T(8,128)}, u32[]{:S(2)}) copy-start(f32[12,256]{1,0:T(8,128)} %fusion.12) | copy-start | bytes 36868
  87.0 4.8 %copy-start.17 = (f32[12,256]{1,0:T(8,128)S(1)}, f32[12,256]{1,0:T(8,128)}, u32[]{:S(2)}) copy-start(f32[12,256]{1,0:T(8,128)} %fusion.16) | copy-start | bytes 36868
  94.9 4.5 %copy-start.4 = (bf16[512,3,256]{2,0,1:T(8,128)(2,1)S(1)}, bf16[512,3,256]{2,0,1:T(8,128)(2,1)}, u32[]{:S(2)}) copy-start(bf16[512,3,256]{2,0,1:T(8,128)(2,1)} %param.15) | copy-start | bytes 2359300
  95.9 15.1 %all-to-all-start.1 = ((bf16[128,4,768]{2,0,1:T(8,128)(2,1)}), bf16[128,4,768]{2,0,1:T(8,128)(2,1)S(1)}, u32[]{:S(2)}, u32[]{:S(2)}) async-start(bf16[128,4,768]{2,0,1:T(8,128)(2,1)} %copy.56), calls=%async_computation.1 | async-start | bytes 1572864 | tf_op jit(solution)/shard_map/all_to_all | solution.py:146
  100.8 10.2 %copy-start.21 = (f32[512]{0:T(512)S(1)}, f32[512]{0:T(512)}, u32[]{:S(2)}) copy-start(f32[512]{0:T(512)} %param.13) | copy-start | bytes 6148
  102.6 9.1 %copy-start.5 = (bf16[512,3,256]{0,2,1:T(8,128)(2,1)S(1)}, bf16[512,3,256]{0,2,1:T(8,128)(2,1)}, u32[]{:S(2)}) copy-start(bf16[512,3,256]{0,2,1:T(8,128)(2,1)} %copy.48) | copy-start | bytes 2359300
  102.6 9.1 %copy-start.20 = (bf16[512,512]{1,0:T(8,128)(2,1)S(1)}, bf16[512,512]{1,0:T(8,128)(2,1)}, u32[]{:S(2)}) copy-start(bf16[512,512]{1,0:T(8,128)(2,1)} %param.14) | copy-start | bytes 1572868
  111.6 1.4 copy-start.22
  111.7 2.0 copy-start.2
  113.0 2.1 copy-start.6
  115.1 15.6 %all-to-all-start.2 = ((bf16[4,128,768]{2,1,0:T(8,128)(2,1)}), bf16[4,128,768]{2,1,0:T(8,128)(2,1)S(1)}, u32[]{:S(2)}, u32[]{:S(2)}) async-start(bf16[4,128,768]{2,1,0:T(8,128)(2,1)} %bitcast.158), calls=%async_computation.2 | async-start | bytes 1572864 | tf_op jit(solution)/shard_map/all_to_all | solution.py:174
  118.6 55.3 %all-reduce.7.cloned.1.call-start = ((), (), s32[]{:S(2)}) async-start(), calls=%async_computation.5 | async-start | bytes 4194304 | tf_op jit(solution)/shard_map/psum | solution.py:175
  118.9 2.8 copy-start.23
  123.4 162.4 %all-reduce.5.cloned.1.call-start = ((), (), s32[]{:S(2)}) async-start(), calls=%async_computation.4 | async-start | bytes 4194304 | tf_op jit(solution)/shard_map/psum | solution.py:175
  131.3 3.7 %copy-start.14 = (f32[12,3840]{1,0:T(8,128)S(1)}, f32[12,3840]{1,0:T(8,128)}, u32[]{:S(2)}) copy-start(f32[12,3840]{1,0:T(8,128)} %get-tuple-element.33) | copy-start | bytes 552964
  131.6 8.8 %slice-start = ((s8[7864320]{0:T(1024)(128)(4,1)}), s8[3670016]{0:T(1024)(128)(4,1)S(1)}, s32[]{:S(2)}) async-start(s8[7864320]{0:T(1024)(128)(4,1)} %bitcast.149), calls=%async_computation.6 | async-start | bytes 7340032
  135.0 2.7 copy-start.13
  135.0 5.4 %slice-start.1 = ((s8[7864320]{0:T(1024)(128)(4,1)}), s8[4194304]{0:T(1024)(128)(4,1)S(1)}, s32[]{:S(2)}) async-start(s8[7864320]{0:T(1024)(128)(4,1)} %bitcast.149), calls=%async_computation.7 | async-start | bytes 8388608
  137.8 2.6 copy-start.12
  140.4 1.0 copy-start.11
  174.1 18.9 %copy-start.19 = (s32[512,1]{0,1:T(1,128)S(1)}, s32[512,1]{0,1:T(1,128)}, u32[]{:S(2)}) copy-start(s32[512,1]{0,1:T(1,128)} %copy-done.18) | copy-start | bytes 6148
  174.1 6.6 %collective-permute-start.2 = (f32[32,1280]{1,0:T(8,128)S(1)}, f32[32,1280]{1,0:T(8,128)S(1)}, u32[]{:S(2)}, u32[]{:S(2)}) collective-permute-start(f32[32,1280]{1,0:T(8,128)S(1)} %get-tuple-element.31), channel_id=1, source_target_pairs={{0,4},{4,8},{8,12},{12,16},{16,20},{20,24},{24,28},{1,5},{5,9},{9,... | collective-permute-start | bytes 491528 | tf_op jit(solution)/shard_map/ppermute | solution.py:18
  177.5 7.3 %collective-permute-start.3 = (f32[32,1280]{1,0:T(8,128)S(1)}, f32[32,1280]{1,0:T(8,128)S(1)}, u32[]{:S(2)}, u32[]{:S(2)}) collective-permute-start(f32[32,1280]{1,0:T(8,128)S(1)} %get-tuple-element.32), channel_id=1, source_target_pairs={{4,0},{8,4},{12,8},{16,12},{20,16},{24,20},{28,24},{5,1},{9,5},{13... | collective-permute-start | bytes 491528 | tf_op jit(solution)/shard_map/ppermute | solution.py:20
  185.8 36.2 %all-to-all-start.3 = ((f32[32,8,160]{2,0,1:T(8,128)}), f32[32,8,160]{2,0,1:T(8,128)S(1)}, u32[]{:S(2)}, u32[]{:S(2)}) async-start(f32[32,8,160]{2,0,1:T(8,128)} %copy.63), calls=%async_computation.3 | async-start | bytes 524288 | tf_op jit(solution)/shard_map/all_to_all | solution.py:180
  285.8 2.4 copy-start.3
Sparse Core Ops, SparseCore 0:
  123.5 50.4 all-reduce.6
  177.6 108.0 all-reduce.4
